TPU v7x, 256 devices: a whole 4x4x8 slice. The times are simulated.
256 devices in a mesh: aux: 64 (over x, z, core), pair: 4 (over y).
Axes of the slice: x: 4, y: 4, z: 8, core: 2. Of those that a mesh axis runs over, the one named last changes fastest.
Arguments:
- shell_ints: bfloat16 [16384, 16, 64, 64], P('aux', 'pair'), may hold values from -0.119628906 to 0.119628906
- block_ids: int32 [16, 2], P('pair'), may hold values from 0 to 15
- block_count: int32 [4], P('pair'), may hold values from 1 to 4, 10 in all
- occ_coef: bfloat16 [16, 64, 512], replicated, may hold values from -0.75 to 0.75
- occ_pick: int32 [512], replicated, may hold values from 0 to 511, each once
- vir_coef: bfloat16 [16, 64, 384], replicated, may hold values from -0.1875 to 0.1875
- occ_energy: float32 [512], replicated, may hold values from -1.5 to -0.3
- vir_energy: float32 [384], replicated, may hold values from 0.2 to 3
Outputs:
- pair_energy: float32 [64], P('aux')
- vir_density: float32 [384, 384], P('pair')
Inputs may be any that keep to these rules, and one draw needn't show every extreme that they name: `block_ids`: basis block numbers of the mu and nu side. `block_count`: the busiest group holds exactly 4 live blocks. `occ_pick`: each of the 512 numbers appears once.
All inputs are finite; a program needn't handle non-finite values.
Results may differ from a plain program's by a relative error of at most 0.01.
Values may be sent and summed in bfloat16 or wider, within the bound.
A program may use at most 128 MiB of HBM per device.

v0:
```python
import jax
import jax.numpy as jnp
from jax import lax
from jax.sharding import PartitionSpec as P


def shifted(value, axis, steps):
    count = lax.axis_size(axis)
    pairs = [(source, (source + steps) % count) for source in range(count)]
    return lax.ppermute(value, axis, pairs)


def group_part(half, vir_rows, nrows):
    slots, width, virtual = vir_rows.shape
    orbitals = half.shape[1]
    flat = half.reshape(nrows, orbitals, slots * width)
    total = jnp.einsum(
        "qik,ka->qia",
        flat,
        vir_rows.reshape(slots * width, virtual),
        preferred_element_type=jnp.float32,
    )
    return lax.optimization_barrier(total.astype(jnp.bfloat16)).astype(jnp.float32)


def slot_tables(ids, live, occ_coef, vir_coef, picker):
    blocks = jnp.arange(occ_coef.shape[0], dtype=jnp.int32)
    nu_onehot = (ids[:, 1][:, None] == blocks[None, :]).astype(jnp.bfloat16)
    mu_onehot = (ids[:, 0][:, None] == blocks[None, :]).astype(jnp.bfloat16) * live[:, None]
    occ_rows = jnp.einsum(
        "kt,tno->kno", nu_onehot, occ_coef, preferred_element_type=jnp.float32
    ).astype(jnp.bfloat16)
    occ_sel = jnp.einsum(
        "kno,oi->kni", occ_rows, picker, preferred_element_type=jnp.float32
    ).astype(jnp.bfloat16)
    vir_rows = jnp.einsum(
        "kt,tma->kma", mu_onehot, vir_coef, preferred_element_type=jnp.float32
    ).astype(jnp.bfloat16)
    return (occ_sel, vir_rows)


def per_device(
    shell_ints, block_ids, block_count, occ_coef, occ_pick, vir_coef, occ_energy, vir_energy
):
    aux_rows, slots, width, _ = shell_ints.shape
    n_aux = lax.axis_size("aux")
    n_pair = lax.axis_size("pair")
    nocc = occ_coef.shape[2]
    virtual = vir_coef.shape[2]
    batch = occ_pick[:n_aux]
    levels = jnp.arange(nocc, dtype=jnp.int32)
    picker = (levels[:, None] == batch[None, :]).astype(jnp.bfloat16)
    live = (jnp.arange(slots, dtype=jnp.int32) < block_count[0]).astype(jnp.bfloat16)
    occ_sel, vir_rows = slot_tables(block_ids, live, occ_coef, vir_coef, picker)
    half = jnp.einsum(
        "qkmn,kni->qikm", shell_ints, occ_sel, preferred_element_type=jnp.float32
    ).astype(jnp.bfloat16)
    partial_value = group_part(half, vir_rows, aux_rows).astype(jnp.bfloat16)
    moved = lax.all_to_all(partial_value, "aux", split_axis=1, concat_axis=0, tiled=True)
    fitted = lax.psum_scatter(
        moved.astype(jnp.float32).astype(jnp.bfloat16), "pair", scatter_dimension=0, tiled=True
    )
    index = lax.axis_index("aux")
    own_rows = fitted[:, 0, :]
    mate_rows = shifted(own_rows, "aux", n_aux // 2)
    block = jnp.einsum("qa,qb->ab", own_rows, mate_rows, preferred_element_type=jnp.float32)
    coulomb = lax.psum(block.astype(jnp.bfloat16), "pair").astype(jnp.float32)
    mate = (index - n_aux // 2) % n_aux
    own_level = jnp.sum(jnp.where(levels == batch[index], occ_energy, 0.0))
    mate_level = jnp.sum(jnp.where(levels == batch[mate], occ_energy, 0.0))
    denom = own_level + mate_level - vir_energy[:, None] - vir_energy[None, :]
    amplitude = coulomb / denom
    energy = jnp.sum(amplitude * (2.0 * coulomb - coulomb.T)).reshape(1)
    share = virtual // n_pair
    first_row = lax.axis_index("pair") * share
    upper = lax.dynamic_slice_in_dim(amplitude, first_row, share, 0)
    column = lax.dynamic_slice_in_dim(amplitude, first_row, share, 1)
    left_rows = 2.0 * upper - column.T
    density_rows = jnp.dot(left_rows, amplitude.T, precision=lax.Precision.HIGHEST)
    vir_density = lax.psum(density_rows, "aux")
    return (energy, vir_density)


def solution(mesh):
    placed = (P("aux", "pair", None, None), P("pair", None), P("pair"), P(), P(), P(), P(), P())
    return jax.shard_map(
        per_device,
        mesh=mesh,
        in_specs=placed,
        out_specs=(P("aux"), P("pair", None)),
        check_vma=False,
    )
```

profile of v0, /device:TPU:1, one launch (start us, length us, event | category | flops | bytes accessed | tf_op | source)
XLA Modules:
  0.0 760.6 jit_solution(14656463893109439184)
XLA Ops:
  7.2 0.0 copy-start
  7.2 0.0 reduce-scatter.2.cloned.1.call-start
  7.2 0.8 slice_bitcast_fusion
  8.0 0.7 slice.10
  9.3 0.0 copy-done
  9.4 0.7 fusion.3
  10.0 0.0 copy-start.1
  10.1 9.2 %fusion.9 = bf16[4,64,256,64]{2,1,3,0:T(8,128)(2,1)} fusion(bf16[256,4,64,64]{0,3,2,1:T(8,128)(2,1)} %param.8, bf16[4,64,512]{2,0,1:T(4,128)(2,1)S(1)} %fusion.3, s32[64]{0:T(128)S(1)} %slice.10), kind=kOutput, calls=%fused_computation.14 | convolution fusion | flops 553697280 | bytes 17039616 | tf_op jit(solution)/shard_map/qkmn,kni->qikm/dot_general | solution.py:55
  19.3 0.0 copy-done.1
  19.3 0.5 fusion.5
  19.8 26.9 %bitcast_convert_fusion = bf16[256,64,384]{2,0,1:T(8,128)(2,1)} fusion(bf16[4,64,256,64]{2,1,3,0:T(8,128)(2,1)} %fusion.9, bf16[4,64,384]{2,0,1:T(4,128)(2,1)S(1)} %fusion.5), kind=kOutput, calls=%fused_computation | convolution fusion | flops 3227516928 | bytes 21168128 | tf_op jit(solution)/shard_map/qik,ka->qia/dot_general | solution.py:17
  46.7 289.0 %all_to_all.18 = bf16[256,64,384]{2,0,1:T(8,128)(2,1)} all-to-all(bf16[256,64,384]{2,0,1:T(8,128)(2,1)} %bitcast_convert_fusion), channel_id=1, replica_groups=mesh['aux'=64,'pair'=4] {'aux'}, dimensions={1} | all-to-all | bytes 25165824 | tf_op jit(solution)/shard_map/all_to_all | solution.py:59
  335.8 0.0 copy-start.3
  335.8 0.0 copy-start.2
  335.8 0.0 reduce-scatter.2.cloned.1.call-update
  335.8 0.0 all-reduce.3.cloned.1.call-start
  335.8 113.9 %reduce-scatter.2.cloned.1.call-done = bf16[4096,1,384]{2,0,1:T(8,128)(2,1)} async-done(((bf16[16384,1,384]{2,0,1:T(8,128)(2,1)}), bf16[4096,1,384]{2,0,1:T(8,128)(2,1)}) %reduce-scatter.2.cloned.1.call-update) | async-done | bytes 3145744 | tf_op jit(solution)/shard_map/reduce_scatter | solution.py:60
  449.7 2.7 collective-permute-start
  452.4 0.6 fusion.34
  453.0 67.5 %collective-permute-done = bf16[4096,384]{1,0:T(8,128)(2,1)} collective-permute-done((bf16[4096,384]{1,0:T(8,128)(2,1)}, bf16[4096,384]{1,0:T(8,128)(2,1)}, u32[]{:S(2)}, u32[]{:S(2)}) %collective-permute-start) | collective-permute-done | bytes 3145760 | tf_op jit(solution)/shard_map/ppermute | solution.py:10
  520.5 5.4 convolution_convert_fusion
  525.9 0.0 all-reduce.3.cloned.1.call-update
  525.9 0.0 all-reduce.5.cloned.1.call-start
  526.0 0.0 copy-done.3
  526.0 2.0 select_reduce_fusion
  529.4 0.0 copy-done.2
  529.4 42.2 %all-reduce.3.cloned.1.call-done = bf16[384,384]{1,0:T(8,128)(2,1)} async-done(((bf16[384,384]{1,0:T(8,128)(2,1)}), bf16[384,384]{1,0:T(8,128)(2,1)}) %all-reduce.3.cloned.1.call-update) | async-done | bytes 294928 | tf_op jit(solution)/shard_map/psum | solution.py:67
  571.5 1.1 copy.10
  572.7 1.9 subtract_divide_fusion
  574.5 0.1 constant_dynamic-slice_fusion
  574.6 0.1 copy.20
  574.8 1.2 fusion.15
  575.9 0.0 all-reduce.5.cloned.1.call-update
  576.0 176.5 %all-reduce.5.cloned.1.call-done = f32[96,384]{1,0:T(8,128)} async-done(((f32[96,384]{1,0:T(8,128)}), f32[96,384]{1,0:T(8,128)}) %all-reduce.5.cloned.1.call-update) | async-done | bytes 147472 | tf_op jit(solution)/shard_map/psum | solution.py:80
  752.5 1.6 copy.39
  (2 shorter events, 0.0 us)
Async XLA Ops:
  7.2 2.2 copy-start
  7.2 442.5 %reduce-scatter.2.cloned.1.call-start = ((), (), s32[]{:S(2)}) async-start(), calls=%async_computation.2 | async-start | bytes 15728640 | tf_op jit(solution)/shard_map/reduce_scatter | solution.py:60
  10.0 9.2 %copy-start.1 = (bf16[16,64,384]{2,1,0:T(8,128)(2,1)S(1)}, bf16[16,64,384]{2,1,0:T(8,128)(2,1)}, u32[]{:S(2)}) copy-start(bf16[16,64,384]{2,1,0:T(8,128)(2,1)} %param.13) | copy-start | bytes 2359300
  335.8 190.2 %copy-start.3 = (f32[512]{0:T(512)S(1)}, f32[512]{0:T(512)}, u32[]{:S(2)}) copy-start(f32[512]{0:T(512)} %param.14) | copy-start | bytes 6148
  335.8 193.6 %copy-start.2 = (f32[384]{0:T(512)S(1)}, f32[384]{0:T(512)}, u32[]{:S(2)}) copy-start(f32[384]{0:T(512)} %param.15) | copy-start | bytes 4612
  335.8 235.7 %all-reduce.3.cloned.1.call-start = ((), (), s32[]{:S(2)}) async-start(), calls=%async_computation.3 | async-start | bytes 589824 | tf_op jit(solution)/shard_map/psum | solution.py:67
  449.7 70.8 %collective-permute-start = (bf16[4096,384]{1,0:T(8,128)(2,1)}, bf16[4096,384]{1,0:T(8,128)(2,1)}, u32[]{:S(2)}, u32[]{:S(2)}) collective-permute-start(bf16[4096,384]{1,0:T(8,128)(2,1)} %bitcast.55), channel_id=1, source_target_pairs={{0,128},{4,132},{8,136},{12,140},{16,144},{20,148},{24,152},{28,15... | collective-permute-start | bytes 9437192 | tf_op jit(solution)/shard_map/ppermute | solution.py:10
  525.9 226.6 %all-reduce.5.cloned.1.call-start = ((), (), s32[]{:S(2)}) async-start(), calls=%async_computation.4 | async-start | bytes 294912 | tf_op jit(solution)/shard_map/psum | solution.py:80
Sparse Core Ops, SparseCore 0:
  335.9 113.7 reduce-scatter.1
  526.1 45.4 all-reduce.2
  576.1 176.3 all-reduce.4
where the time goes:
time: 761 us
  waiting for transfers between devices  400 us (53%)
  blocking collectives  289 us (38%)
  matrix products  43.9 us (6%)
  between operations  15.8 us (2%)
    all_to_all x1, blocking collectives, per_device(): lax.all_to_all(partial_value, 'aux', split_axis=1, concat_axis=0, tiled=T...  289 us
    psum x1, waiting for transfers between devices, per_device(): vir_density = lax.psum(density_rows, 'aux')  177 us
    reduce_scatter x1, waiting for transfers between devices, per_device(): lax.psum_scatter(moved.astype(jnp.float32).astype(jnp.bfloat16), 'pair',...  114 us
    ppermute x1, waiting for transfers between devices, shifted(): return lax.ppermute(value, axis, pairs)  67.5 us
    psum x1, waiting for transfers between devices, per_device(): coulomb = lax.psum(block.astype(jnp.bfloat16), 'pair').astype(jnp.float32)  42.2 us
    dot_general x1, matrix products, group_part(): jnp.einsum('qik,ka->qia', flat, vir_rows.reshape(slots * width, virtual),...  26.9 us
  transfers between devices with their start and end apart: 4, of which 4 were waited for; matrix products, arithmetic and copies ran while one was open for 0% of the time, Pallas kernels for 0%

commit v1 on v0

v1 whole, which is shorter than its diff:
```python
import functools

import jax
import jax.numpy as jnp
from jax import lax
from jax.experimental import pallas as pl
from jax.experimental.pallas import tpu as pltpu
from jax.sharding import PartitionSpec as P

F32, BF16, I32 = jnp.float32, jnp.bfloat16, jnp.int32
MESH = pl.DeviceIdType.MESH
NX, NY, NZ, NC = 4, 4, 8, 2
NT = (((1,), (1,)), ((), ()))
DMA = pltpu.SemaphoreType.DMA


def dot(a, b, dims=(((1,), (0,)), ((), ()))):
    return lax.dot_general(a, b, dims, preferred_element_type=F32)


def onehot(mask):
    return jnp.where(mask, 1.0, 0.0).astype(BF16)


def iota(shape, axis):
    return lax.broadcasted_iota(I32, shape, axis)


def kernel(
    ids, count, pick_s, eocc,
    ints_hbm, occ, pick_v, vir, evir,
    out_d, out_e,
    ints, lhs, half, vir_t, vt, meta, meta_in,
    far, near, relay, part,
    cbuf, core_in, x_in, zsum, z_in, call, amp, amp_t, mix,
    dblk, d_in, dy, p2_in, p3, fin,
    ints_sem, meta_ss, meta_rs, far_ss, far_rs, near_ss, near_rs, part_ss, part_rs,
    core_ss, core_rs, x_ss, x_rs, z_ss, z_rs, ag_ss, ag_rs, y_ss, y_rs,
    p2_ss, p2_rs, p3_ss, p3_rs, f_ss, f_rs,
):
    a = lax.axis_index("aux")
    p = lax.axis_index("pair")
    c = lax.rem(a, NC)
    z = lax.rem(lax.div(a, NC), NZ)
    x = lax.div(a, NC * NZ)

    def dev(px, py, pz, pc):
        return {"aux": (px * NZ + pz) * NC + pc, "pair": py}

    def remote(src, dst, ss, rs, to):
        return pltpu.make_async_remote_copy(
            src_ref=src, dst_ref=dst, send_sem=ss, recv_sem=rs, device_id=to, device_id_type=MESH
        )

    def ypeer(step):
        return dev(x, lax.rem(p + step + NY, NY), z, c)

    loads = [pltpu.make_async_copy(ints_hbm.at[s], ints.at[s], ints_sem.at[s]) for s in range(4)]
    for load in loads:
        load.start()

    barrier = pltpu.get_barrier_semaphore()

    def greet(to):
        pl.semaphore_signal(barrier, inc=1, device_id=to, device_id_type=MESH)

    for step in range(1, NY):
        greet(ypeer(step))

    def greet_xc(o, carry):
        s = lax.rem(x * NC + c + o, NX * NC)
        greet(dev(lax.div(s, NC), p, z, lax.rem(s, NC)))
        return carry

    lax.fori_loop(1, NX * NC, greet_xc, 0)

    def greet_z(o, carry):
        pz = lax.rem(z + o, NZ)
        greet(dev(x, p, pz, 0))
        greet(dev(x, p, pz, 1))
        return carry

    lax.fori_loop(1, NZ, greet_z, 0)

    lane = iota((8, 256), 1)
    slot = lax.shift_right_logical(lane, 6)
    mine = jnp.full((8, 256), ids[0, 0], I32)
    for k in range(1, 4):
        mine = jnp.where(slot == k, ids[k, 0], mine)
    meta[...] = jnp.where(slot < count[0], mine * 64 + (lane & 63), -1)

    pick_t = onehot(iota((512, 64), 0) == pick_v[:, 0:64])
    r = iota((512, 64), 0)
    orbital = (lax.shift_right_logical(r, 3) & 1) * 32 + (lax.shift_right_logical(r, 4) & 3) * 8
    orbital = orbital + lax.shift_right_logical(r, 6)
    pick_e = dot(onehot(iota((512, 64), 1) == orbital), pick_t, NT).astype(BF16)
    same = (iota((512, 512), 0) & 7) == lax.shift_right_logical(iota((512, 512), 1), 6)

    def make_lhs(s, carry):
        rows = occ[ids[s, 1]]
        tiled = jnp.concatenate([rows] * 8, axis=0)
        lhs[s] = jnp.where(same, dot(pick_e, tiled, NT), 0.0).astype(BF16)
        return carry

    lax.fori_loop(0, 4, make_lhs, 0)

    pl.semaphore_wait(barrier, 3 + 7 + 14)

    metas = [
        remote(meta, meta_in.at[0], meta_ss.at[0], meta_rs.at[0], ypeer(-1)),
        remote(meta, meta_in.at[1], meta_ss.at[1], meta_rs.at[1], ypeer(1)),
    ]
    for m in metas:
        m.start()
    for load in loads:
        load.wait()

    def far_copy(j, d):
        t = lax.rem(p + 2, NY)
        return remote(half.at[pl.ds(j * 8 + t * 2, 2)], far.at[j], far_ss.at[j], far_rs.at[j], ypeer(d))

    def near_copy(j, d):
        t = lax.rem(p - d + NY, NY)
        return remote(half.at[pl.ds(j * 8 + t * 2, 2)], near.at[j], near_ss.at[j], near_rs.at[j], ypeer(-d))

    def part_copy(j, d):
        return remote(relay.at[j], part.at[j], part_ss.at[j], part_rs.at[j], ypeer(d))

    def half_pass(q, carry):
        def one_slot(s, inner):
            rows = lhs[s, pl.ds(pl.multiple_of(q * 128, 128), 128), :]
            for h in range(4):
                u = dot(rows, ints[s, 2 * h]).reshape(16, 8, 256)
                v = dot(rows, ints[s, 2 * h + 1]).reshape(16, 8, 256)
                block = jnp.concatenate([u, v], axis=1).astype(BF16)
                half[pl.ds(q * 16, 16), pl.ds(pl.multiple_of(s * 64 + h * 16, 16), 16), :] = block
            return inner

        lax.fori_loop(0, 4, one_slot, 0)
        far_copy(2 * q, 1).start()
        far_copy(2 * q + 1, -1).start()
        near_copy(2 * q, 1).start()
        near_copy(2 * q + 1, -1).start()
        return carry

    lax.fori_loop(0, 4, half_pass, 0)

    vir_t[...] = vir[...].astype(F32).T.astype(BF16)
    row = iota((1024, 256), 0)
    vt[0] = dot(vir_t[...], onehot(row == meta[0:1, :])).astype(BF16)
    for g in range(2):
        metas[g].wait_recv()
        vt[1 + g] = dot(vir_t[...], onehot(row == meta_in[g, 0:1, :])).astype(BF16)

    def do_relay(j, d):
        far_copy(j, d).wait_recv()
        t = lax.rem(p + d + NY, NY)
        for gh in range(2):
            total = dot(vt[2 if d == 1 else 1], far[j, gh]) + dot(vt[0], half[j * 8 + t * 2 + gh])
            relay[j, gh] = total.astype(BF16)
        part_copy(j, d).start()

    def relay_pass(q, carry):
        do_relay(2 * q, 1)
        do_relay(2 * q + 1, -1)
        return carry

    lax.fori_loop(0, 4, relay_pass, 0)

    def core_copy(j):
        return remote(cbuf.at[j, 1 - c], core_in.at[j], core_ss.at[j], core_rs.at[j], dev(x, p, z, 1 - c))

    def x_copy(j, o):
        q = lax.rem(x + o, NX)
        return remote(
            core_in.at[j, q], x_in.at[j, o - 1], x_ss.at[j, o - 1], x_rs.at[j, o - 1], dev(q, p, z, c)
        )

    def z_copy(j, o):
        return remote(zsum.at[j], z_in.at[o - 1], z_ss.at[j], z_rs.at[o - 1], dev(x, p, j, c))

    def do_target(j, d):
        near_copy(j, d).wait_recv()
        part_copy(j, d).wait_recv()
        fitted = []
        for gh in range(2):
            total = part[j, gh].astype(F32) + dot(vt[1 if d == 1 else 2], near[j, gh])
            total = total + dot(vt[0], half[j * 8 + p * 2 + gh])
            fitted.append(total.astype(BF16))
        block = dot(fitted[0], fitted[1], NT)
        for q in range(4):
            for pc in range(2):
                lo = q * 96 + pc * 48
                cbuf[j, pc, q] = block[lo : lo + 48]
        core_copy(j).start()

    def do_core(j):
        core_copy(j).wait_recv()
        core_in[j] = core_in[j] + cbuf[j, c]
        for o in range(1, NX):
            x_copy(j, o).start()

    def do_x(j):
        total = core_in[j, x]
        for o in range(1, NX):
            x_copy(j, o).wait_recv()
            total = total + x_in[j, o - 1]
        zsum[j] = total

        @pl.when(z != j)
        def _():
            z_copy(j, lax.rem(z - j + NZ, NZ)).start()

    def target_pass(q, carry):
        do_target(2 * q, 1)

        @pl.when(q > 0)
        def _():
            do_core(2 * q - 1)
            do_x(2 * q - 2)

        do_target(2 * q + 1, -1)
        do_core(2 * q)

        @pl.when(q > 0)
        def _():
            do_x(2 * q - 1)

        return carry

    lax.fori_loop(0, 4, target_pass, 0)
    do_core(7)
    do_x(6)
    do_x(7)

    total = zsum[z]
    for o in range(1, NZ):
        z_copy(z, o).wait_recv()
        total = total + z_in[o - 1]
    slab = x * NC + c
    call[slab] = total

    def ag_copy(o, src):
        s = lax.rem(slab + o, NX * NC)
        to = dev(lax.div(s, NC), p, z, lax.rem(s, NC))
        return remote(call.at[src], call.at[src], ag_ss.at[o - 1], ag_rs.at[src], to)

    for o in range(1, NX * NC):
        ag_copy(o, slab).start()
    for o in range(1, NX * NC):
        ag_copy(o, lax.rem(slab + o, NX * NC)).wait_recv()

    k = p * NZ + z
    level = eocc[pick_s[k]] + eocc[pick_s[k + 32]]
    block = call[...].reshape(384, 384)
    block_t = block.T
    across = jnp.broadcast_to(evir[...], (384, 384))
    denom = level - across.T - across
    amplitude = block / denom
    energy = jnp.sum(amplitude * (2.0 * block - block_t))
    amplitude_t = block_t / denom
    first = c == 0
    amp[...] = jnp.where(first, amplitude, amplitude_t)
    mix[...] = jnp.where(first, 2.0 * amplitude - amplitude_t, 2.0 * amplitude_t - amplitude)
    rows = jnp.concatenate([mix[pl.ds(pl.multiple_of(y * 96 + x * 24, 8), 24), :] for y in range(4)], axis=0)
    share = lax.dot_general(rows, amp[...], NT, precision=lax.Precision.HIGHEST, preferred_element_type=F32)
    tip = jnp.where((iota((8, 384), 1) == k) & first, energy, 0.0)
    for y in range(4):
        dblk[y, 0:24, :] = share[y * 24 : y * 24 + 24]
        dblk[y, 24:32, :] = tip

    def y_copy(o):
        y = lax.rem(p + o, NY)
        return remote(dblk.at[y], d_in.at[o - 1], y_ss.at[o - 1], y_rs.at[o - 1], dev(x, y, z, c))

    for o in range(1, NY):
        y_copy(o).start()
    total = dblk[p]
    for o in range(1, NY):
        y_copy(o).wait_recv()
        total = total + d_in[o - 1]
    dy[...] = total.reshape(4, 8, 384)

    line = z * NC + c

    def p2_copy(t, src):
        return remote(dy.at[t], p2_in.at[src], p2_ss.at[t], p2_rs.at[src], dev(x, p, 2 * t, 0))

    for t in range(4):

        @pl.when(line != 4 * t)
        def _():
            p2_copy(t, line).start()

    root = lax.rem(line, 4) == 0
    mytile = lax.div(line, 4)

    def p3_copy(o, src):
        return remote(p3.at[src], p3.at[src], p3_ss.at[o - 1], p3_rs.at[src], dev(lax.rem(x + o, NX), p, z, c))

    def f_copy(o, tile):
        to = lax.rem(line + o, NZ * NC)
        return remote(fin.at[tile], fin.at[tile], f_ss.at[o - 1], f_rs.at[tile], dev(x, p, lax.div(to, NC), lax.rem(to, NC)))

    @pl.when(root)
    def _():
        p2_in[line] = dy[mytile]

        def arrive(o, carry):
            p2_copy(0, lax.rem(line + o, NZ * NC)).wait_recv()
            return carry

        lax.fori_loop(1, NZ * NC, arrive, 0)
        p3[x] = jnp.sum(p2_in[...], axis=0)
        for o in range(1, NX):
            p3_copy(o, x).start()
        for o in range(1, NX):
            p3_copy(o, lax.rem(x + o, NX)).wait_recv()
        fin[mytile] = p3[...]

        def send(o, carry):
            f_copy(o, mytile).start()
            return carry

        lax.fori_loop(1, NZ * NC, send, 0)

    for t in range(4):

        @pl.when(line != 4 * t)
        def _():
            f_copy(1, t).wait_recv()

    for q in range(4):
        for t in range(3):
            out_d[q * 24 + t * 8 : q * 24 + t * 8 + 8, :] = fin[t, q]
    mine_e = fin[3, 0][0:1, :]
    out_e[0] = jnp.sum(jnp.where(iota((1, 384), 1) == lax.rem(a, 32), mine_e, 0.0))

    for m in metas:
        m.wait_send()

    def sent(q, carry):
        for j, d in ((2 * q, 1), (2 * q + 1, -1)):
            far_copy(j, d).wait_send()
            near_copy(j, d).wait_send()
            part_copy(j, d).wait_send()
            core_copy(j).wait_send()
            for o in range(1, NX):
                x_copy(j, o).wait_send()

            @pl.when(z != j)
            def _():
                z_copy(j, 1).wait_send()

        return carry

    lax.fori_loop(0, 4, sent, 0)
    for o in range(1, NX * NC):
        ag_copy(o, slab).wait_send()
    for o in range(1, NY):
        y_copy(o).wait_send()
    for t in range(4):

        @pl.when(line != 4 * t)
        def _():
            p2_copy(t, line).wait_send()

    @pl.when(root)
    def _():
        for o in range(1, NX):
            p3_copy(o, x).wait_send()

        def done(o, carry):
            f_copy(o, mytile).wait_send()
            return carry

        lax.fori_loop(1, NZ * NC, done, 0)


def per_device(
    shell_ints, block_ids, block_count, occ_coef, occ_pick, vir_coef, occ_energy, vir_energy
):
    ints = jnp.transpose(shell_ints, (1, 2, 3, 0)).reshape(4, 8, 512, 256)
    smem = pl.BlockSpec(memory_space=pltpu.SMEM)
    vmem = pl.BlockSpec(memory_space=pltpu.VMEM)
    density, energy = pl.pallas_call(
        kernel,
        out_shape=(jax.ShapeDtypeStruct((96, 384), F32), jax.ShapeDtypeStruct((1,), F32)),
        in_specs=[smem] * 4 + [pl.BlockSpec(memory_space=pl.ANY)] + [vmem] * 4,
        out_specs=(vmem, smem),
        scratch_shapes=[
            pltpu.VMEM((4, 8, 512, 256), BF16),
            pltpu.VMEM((4, 512, 512), BF16),
            pltpu.VMEM((64, 256, 256), BF16),
            pltpu.VMEM((384, 1024), BF16),
            pltpu.VMEM((3, 384, 256), BF16),
            pltpu.VMEM((8, 256), I32),
            pltpu.VMEM((2, 8, 256), I32),
            pltpu.VMEM((8, 2, 256, 256), BF16),
            pltpu.VMEM((8, 2, 256, 256), BF16),
            pltpu.VMEM((8, 2, 384, 256), BF16),
            pltpu.VMEM((8, 2, 384, 256), BF16),
            pltpu.VMEM((8, 2, 4, 48, 384), F32),
            pltpu.VMEM((8, 4, 48, 384), F32),
            pltpu.VMEM((8, 3, 48, 384), F32),
            pltpu.VMEM((8, 48, 384), F32),
            pltpu.VMEM((7, 48, 384), F32),
            pltpu.VMEM((8, 48, 384), F32),
            pltpu.VMEM((384, 384), F32),
            pltpu.VMEM((8, 128), F32),
            pltpu.VMEM((384, 384), F32),
            pltpu.VMEM((4, 32, 384), F32),
            pltpu.VMEM((3, 32, 384), F32),
            pltpu.VMEM((4, 8, 384), F32),
            pltpu.VMEM((16, 8, 384), F32),
            pltpu.VMEM((4, 8, 384), F32),
            pltpu.VMEM((4, 4, 8, 384), F32),
            DMA((4,)),
            DMA((2,)), DMA((2,)),
            DMA((8,)), DMA((8,)),
            DMA((8,)), DMA((8,)),
            DMA((8,)), DMA((8,)),
            DMA((8,)), DMA((8,)),
            DMA((8, 3)), DMA((8, 3)),
            DMA((8,)), DMA((7,)),
            DMA((7,)), DMA((8,)),
            DMA((3,)), DMA((3,)),
            DMA((4,)), DMA((16,)),
            DMA((3,)), DMA((4,)),
            DMA((15,)), DMA((4,)),
        ],
        compiler_params=pltpu.CompilerParams(
            collective_id=0, has_side_effects=True, vmem_limit_bytes=56 << 20
        ),
    )(
        block_ids, block_count, occ_pick, occ_energy,
        ints, occ_coef, occ_pick.reshape(1, 512), vir_coef.reshape(1024, 384),
        vir_energy.reshape(1, 384),
    )
    return (energy, density)


def solution(mesh):
    placed = (P("aux", "pair", None, None), P("pair", None), P("pair"), P(), P(), P(), P(), P())
    return jax.shard_map(
        per_device,
        mesh=mesh,
        in_specs=placed,
        out_specs=(P("aux"), P("pair", None)),
        check_vma=False,
    )
```

time: 761 us -> 156 us (0.20)
  waiting for transfers between devices: 400 us -> 0 us
  blocking collectives: 289 us -> 0 us
  Pallas kernels: 0 us -> 149 us
  matrix products: 43.9 us -> 0 us
  between operations: 15.8 us -> 3.05 us
    all_to_all x1 -> x0, blocking collectives: 289 us -> none  [per_device(): lax.all_to_all(partial_value, 'aux', split_axis=1, concat_axis=0, tiled=T...]
    psum x2 -> x0, waiting for transfers between devices: 219 us -> none  [the longest x1 177 us: per_device(): vir_density = lax.psum(density_rows, 'aux')]
    pallas_call x0 -> x1, Pallas kernels: none -> 149 us  [per_device(): pl.pallas_call(kernel, out_shape=(jax.ShapeDtypeStruct((96, 384), F32), j...]
    reduce_scatter x1 -> x0, waiting for transfers between devices: 114 us -> none  [per_device(): lax.psum_scatter(moved.astype(jnp.float32).astype(jnp.bfloat16), 'pair',...]
    ppermute x1 -> x0, waiting for transfers between devices: 67.5 us -> none  [shifted(): return lax.ppermute(value, axis, pairs)]
    dot_general x6 -> x0, matrix products: 43.9 us -> none  [the longest x1 26.9 us: group_part(): jnp.einsum('qik,ka->qia', flat, vir_rows.reshape(slots * width, virtual),...]
  transfers between devices with their start and end apart: 4 -> 0, of which waited for: 4 -> 0; matrix products, arithmetic and copies ran while one was open for 0% -> 0% of each run, Pallas kernels for 0% -> 0%
where the time goes in v1:
time: 156 us
  Pallas kernels  149 us (96%)
  local copies, waits for them, and re-layouts  4.16 us (3%)
  between operations  3.05 us (2%)
    pallas_call x1, Pallas kernels, per_device(): pl.pallas_call(kernel, out_shape=(jax.ShapeDtypeStruct((96, 384), F32), j...  149 us

profile of v1, /device:TPU:1, one launch (start us, length us, event | category | flops | bytes accessed | tf_op | source)
XLA Modules:
  0.0 155.8 jit_solution(16867041292595578963)
XLA Ops:
  1.3 1.2 reshape.19.evir
  2.5 1.3 copy.10.ids
  3.9 148.6 %shard_map.95 = (f32[96,384]{1,0:T(8,128)}, f32[1]{0:T(128)}) custom-call(s32[4,2]{1,0:T(4,128)} %copy.10.ids, s32[1]{0:T(128)S(6)} %copy.13.count, s32[512]{0:T(512)} %pick_s.1, f32[512]{0:T(512)} %eocc.1, bf16[4,8,512,256]{3,2,1,0:T(8,128)(2,1)} %bitcast.5, bf16[16,64,512]{2,1,0:T(8,128)(2,1)} %occ.1, s32[1,512]{1,0:T(1,128)} %bitcast.7, ...), custom_call_target="tpu_custom_call" | custom-call | tf_op jit(solution)/shard_map/pallas_call | solution.py:386
  153.1 1.6 %copy.15 = f32[96,384]{1,0:T(8,128)} copy(f32[96,384]{1,0:T(8,128)} %get-tuple-element.9) | data formatting | bytes 294912

commit v2 on v1

v2 whole, which is shorter than its diff:
```python
import functools

import jax
import jax.numpy as jnp
from jax import lax
from jax.experimental import pallas as pl
from jax.experimental.pallas import tpu as pltpu
from jax.sharding import PartitionSpec as P

F32, BF16, I32 = jnp.float32, jnp.bfloat16, jnp.int32
MESH = pl.DeviceIdType.MESH
NX, NY, NZ, NC = 4, 4, 8, 2
NT = (((1,), (1,)), ((), ()))
DMA = pltpu.SemaphoreType.DMA


def dot(a, b, dims=(((1,), (0,)), ((), ()))):
    return lax.dot_general(a, b, dims, preferred_element_type=F32)


def onehot(mask):
    return jnp.where(mask, 1.0, 0.0).astype(BF16)


def iota(shape, axis):
    return lax.broadcasted_iota(I32, shape, axis)


def kernel(
    ids, count, pick_s, eocc,
    ints_hbm, vir_hbm, occ, pick_v, evir,
    out_d, out_e,
    ints, vir, lhs, half, vir_t, vt, meta, meta_in,
    far, near, relay, part,
    cbuf, core_in, x_out, x_in, zsum, z_out, z_in, call,
    dblk, d_in, dy, zr_in, fin,
    ints_sem, vir_sem, meta_ss, meta_rs, far_ss, far_rs, near_ss, near_rs, part_ss, part_rs,
    core_ss, core_rs, x_ss, x_rs, z_ss, z_rs, ag_ss, ag_rs, y_ss, y_rs,
    zr_ss, zr_rs, zg_ss, zg_rs, f_ss, f_rs,
):
    a = lax.axis_index("aux")
    p = lax.axis_index("pair")
    c = lax.rem(a, NC)
    z = lax.rem(lax.div(a, NC), NZ)
    x = lax.div(a, NC * NZ)

    def dev(px, py, pz, pc):
        return {"aux": (px * NZ + pz) * NC + pc, "pair": py}

    def remote(src, dst, ss, rs, to):
        return pltpu.make_async_remote_copy(
            src_ref=src, dst_ref=dst, send_sem=ss, recv_sem=rs, device_id=to, device_id_type=MESH
        )

    def ypeer(step):
        return dev(x, lax.rem(p + step + NY, NY), z, c)

    loads = [pltpu.make_async_copy(ints_hbm.at[s], ints.at[s], ints_sem.at[s]) for s in range(4)]
    for load in loads:
        load.start()
    vir_load = pltpu.make_async_copy(vir_hbm, vir, vir_sem)
    vir_load.start()

    barrier = pltpu.get_barrier_semaphore()

    def greet(to):
        pl.semaphore_signal(barrier, inc=1, device_id=to, device_id_type=MESH)

    for step in range(1, NY):
        greet(ypeer(step))

    def greet_xc(o, carry):
        s = lax.rem(x * NC + c + o, NX * NC)
        greet(dev(lax.div(s, NC), p, z, lax.rem(s, NC)))
        return carry

    lax.fori_loop(1, NX * NC, greet_xc, 0)

    def greet_z(o, carry):
        pz = lax.rem(z + o, NZ)
        greet(dev(x, p, pz, c))
        return carry

    lax.fori_loop(1, NZ, greet_z, 0)

    lane = iota((8, 256), 1)
    slot = lax.shift_right_logical(lane, 6)
    mine = jnp.full((8, 256), ids[0, 0], I32)
    for k in range(1, 4):
        mine = jnp.where(slot == k, ids[0, k], mine)
    meta[...] = jnp.where(slot < count[0], mine * 64 + (lane & 63), -1)

    pick_t = onehot(iota((512, 64), 0) == pick_v[:, 0:64])
    rows = jnp.concatenate([occ[ids[1, s]] for s in range(4)], axis=0)
    chosen = dot(rows, pick_t).astype(BF16)
    r = iota((512, 64), 0)
    orbital = (lax.shift_right_logical(r, 3) & 1) * 32 + (lax.shift_right_logical(r, 4) & 3) * 8
    orbital = orbital + lax.shift_right_logical(r, 6)
    spread = onehot(iota((512, 64), 1) == orbital)
    same = (iota((512, 512), 0) & 7) == lax.shift_right_logical(iota((512, 512), 1), 6)
    for s in range(4):
        tiled = jnp.concatenate([chosen[s * 64 : s * 64 + 64]] * 8, axis=0)
        lhs[s] = jnp.where(same, dot(spread, tiled, NT), 0.0).astype(BF16)

    pl.semaphore_wait(barrier, 3 + 7 + 7)

    metas = [
        remote(meta, meta_in.at[0], meta_ss.at[0], meta_rs.at[0], ypeer(-1)),
        remote(meta, meta_in.at[1], meta_ss.at[1], meta_rs.at[1], ypeer(1)),
    ]
    for m in metas:
        m.start()
    for load in loads:
        load.wait()

    def way(j):
        return 1 - 2 * (j & 1)

    def far_copy(j):
        t = lax.rem(p + 2, NY)
        return remote(half.at[pl.ds(j * 8 + t * 2, 2)], far.at[j], far_ss.at[j], far_rs.at[j], ypeer(way(j)))

    def near_copy(j):
        t = lax.rem(p - way(j) + NY, NY)
        return remote(half.at[pl.ds(j * 8 + t * 2, 2)], near.at[j], near_ss.at[j], near_rs.at[j], ypeer(-way(j)))

    def part_copy(j):
        return remote(relay.at[j], part.at[j], part_ss.at[j], part_rs.at[j], ypeer(way(j)))

    def half_rows(low, n):
        def one_slot(s, carry):
            rows = lhs[s, low * 8 : (low + n) * 8, :]
            for h in range(4):
                u = dot(rows, ints[s, 2 * h]).reshape(n, 8, 256)
                v = dot(rows, ints[s, 2 * h + 1]).reshape(n, 8, 256)
                block = jnp.concatenate([u, v], axis=1).astype(BF16)
                half[low : low + n, pl.ds(pl.multiple_of(s * 64 + h * 16, 16), 16), :] = block
            return carry

        lax.fori_loop(0, 4, one_slot, 0)
        for j in range(low // 8, (low + n) // 8):
            far_copy(j).start()

    half_rows(0, 16)
    half_rows(16, 48)

    vir_load.wait()
    vir_t[...] = vir[...].astype(F32).T.astype(BF16)
    row = iota((1024, 256), 0)
    vt[0] = dot(vir_t[...], onehot(row == meta[0:1, :])).astype(BF16)
    for g in range(2):
        metas[g].wait_recv()
        vt[1 + g] = dot(vir_t[...], onehot(row == meta_in[g, 0:1, :])).astype(BF16)

    def do_relay(j):
        far_copy(j).wait_recv()
        t = lax.rem(p + way(j) + NY, NY)
        for gh in range(2):
            total = dot(vt[2 - (j & 1)], far[j, gh]) + dot(vt[0], half[j * 8 + t * 2 + gh])
            relay[j, gh] = total.astype(BF16)
        part_copy(j).start()
        near_copy(j).start()

    def core_copy(j):
        return remote(cbuf.at[j, 1 - c], core_in.at[j], core_ss.at[j], core_rs.at[j], dev(x, p, z, 1 - c))

    def x_copy(j, o):
        q = lax.rem(x + o, NX)
        return remote(
            x_out.at[j, q], x_in.at[j, o - 1], x_ss.at[j, o - 1], x_rs.at[j, o - 1], dev(q, p, z, c)
        )

    def z_copy(j, o):
        return remote(z_out.at[j], z_in.at[o - 1], z_ss.at[j], z_rs.at[o - 1], dev(x, p, j, c))

    def do_target(j):
        near_copy(j).wait_recv()
        part_copy(j).wait_recv()
        fitted = []
        for gh in range(2):
            total = part[j, gh].astype(F32) + dot(vt[1 + (j & 1)], near[j, gh])
            total = total + dot(vt[0], half[j * 8 + p * 2 + gh])
            fitted.append(total.astype(BF16))
        block = dot(fitted[0], fitted[1], NT)
        for q in range(4):
            for pc in range(2):
                lo = q * 96 + pc * 48
                cbuf[j, pc, q] = block[lo : lo + 48]
        core_copy(j).start()

    def do_core(j):
        core_copy(j).wait_recv()
        both = core_in[j] + cbuf[j, c]
        core_in[j] = both
        x_out[j] = both.astype(BF16)
        for o in range(1, NX):
            x_copy(j, o).start()

    def do_x(j):
        total = core_in[j, x]
        for o in range(1, NX):
            x_copy(j, o).wait_recv()
            total = total + x_in[j, o - 1].astype(F32)
        zsum[j] = total
        z_out[j] = total.astype(BF16)

        @pl.when(z != j)
        def _():
            z_copy(j, lax.rem(z - j + NZ, NZ)).start()

    def step(n, carry):
        @pl.when(n < 8)
        def _():
            do_relay(n)

        @pl.when(n > 3)
        def _():
            do_core(n - 4)
            do_x(n - 4)

        @pl.when(n > 2)
        def _():
            do_target(n - 3)

        return carry

    lax.fori_loop(0, 11, step, 0)
    do_core(7)
    do_x(7)

    total = zsum[z]
    for o in range(1, NZ):
        z_copy(z, o).wait_recv()
        total = total + z_in[o - 1].astype(F32)
    slab = x * NC + c
    call[slab] = total.astype(BF16)

    def ag_copy(o, src):
        s = lax.rem(slab + o, NX * NC)
        to = dev(lax.div(s, NC), p, z, lax.rem(s, NC))
        return remote(call.at[src], call.at[src], ag_ss.at[o - 1], ag_rs.at[src], to)

    for o in range(1, NX * NC):
        ag_copy(o, slab).start()
    for o in range(1, NX * NC):
        ag_copy(o, lax.rem(slab + o, NX * NC)).wait_recv()

    k = p * NZ + z
    level = eocc[pick_s[k]] + eocc[pick_s[k + 32]]
    block = call[...].astype(F32).reshape(384, 384)
    block_t = block.T
    across = jnp.broadcast_to(evir[...].reshape(1, 384), (384, 384))
    denom = level - across.T - across
    amplitude = block / denom
    energy = jnp.sum(amplitude * (2.0 * block - block_t))
    amplitude_t = block_t / denom

    high = functools.partial(
        lax.dot_general, precision=lax.Precision.HIGHEST, preferred_element_type=F32
    )
    rank = iota((64, 384), 0) & 15
    wanted = lax.shift_right_logical(iota((64, 384), 0), 4) * 96 + slab * 12 + rank
    chosen = jnp.where((iota((64, 384), 1) == wanted) & (rank < 12), 1.0, 0.0)
    plain = (((1,), (0,)), ((), ()))
    share = high(high(chosen, 2.0 * amplitude - amplitude_t, plain), amplitude_t, plain)
    share = share + high(high(chosen, 2.0 * amplitude_t - amplitude, plain), amplitude, plain)
    share = share + jnp.where((iota((64, 384), 1) == k) & (rank == 12), energy, 0.0)
    for y in range(4):
        dblk[y] = share[y * 16 : y * 16 + 16]

    def y_copy(o):
        y = lax.rem(p + o, NY)
        return remote(dblk.at[y], d_in.at[o - 1], y_ss.at[o - 1], y_rs.at[o - 1], dev(x, y, z, c))

    for o in range(1, NY):
        y_copy(o).start()
    total = dblk[p]
    for o in range(1, NY):
        y_copy(o).wait_recv()
        total = total + d_in[o - 1]
    dy[...] = total.reshape(8, 2, 384)

    def zr_copy(o):
        pz = lax.rem(z + o, NZ)
        return remote(dy.at[pz], zr_in.at[o - 1], zr_ss.at[o - 1], zr_rs.at[o - 1], dev(x, p, pz, c))

    def zg_copy(o, src):
        pz = lax.rem(z + o, NZ)
        return remote(fin.at[slab, src], fin.at[slab, src], zg_ss.at[o - 1], zg_rs.at[src], dev(x, p, pz, c))

    def f_copy(o, src):
        to = lax.rem(slab + o, NX * NC)
        return remote(fin.at[src], fin.at[src], f_ss.at[o - 1], f_rs.at[src], dev(lax.div(to, NC), p, z, lax.rem(to, NC)))

    for o in range(1, NZ):
        zr_copy(o).start()
    total = dy[z]
    for o in range(1, NZ):
        zr_copy(o).wait_recv()
        total = total + zr_in[o - 1]
    fin[slab, z] = total
    for o in range(1, NZ):
        zg_copy(o, z).start()
    for o in range(1, NZ):
        zg_copy(o, lax.rem(z + o, NZ)).wait_recv()
    for o in range(1, NX * NC):
        f_copy(o, slab).start()
    for o in range(1, NX * NC):
        f_copy(o, lax.rem(slab + o, NX * NC)).wait_recv()

    out_d[...] = fin[:, 0:6].reshape(96, 384)
    out_e[0] = jnp.sum(jnp.where(iota((1, 384), 1) == lax.rem(a, 32), fin[0, 6][0:1, :], 0.0))

    for m in metas:
        m.wait_send()

    def sent(j, carry):
        far_copy(j).wait_send()
        near_copy(j).wait_send()
        part_copy(j).wait_send()
        core_copy(j).wait_send()
        for o in range(1, NX):
            x_copy(j, o).wait_send()

        @pl.when(z != j)
        def _():
            z_copy(j, 1).wait_send()

        return carry

    lax.fori_loop(0, 8, sent, 0)
    for o in range(1, NX * NC):
        ag_copy(o, slab).wait_send()
        f_copy(o, slab).wait_send()
    for o in range(1, NY):
        y_copy(o).wait_send()
    for o in range(1, NZ):
        zr_copy(o).wait_send()
        zg_copy(o, z).wait_send()


def per_device(
    shell_ints, block_ids, block_count, occ_coef, occ_pick, vir_coef, occ_energy, vir_energy
):
    ints = jnp.transpose(shell_ints, (1, 2, 3, 0)).reshape(4, 8, 512, 256)
    smem = pl.BlockSpec(memory_space=pltpu.SMEM)
    vmem = pl.BlockSpec(memory_space=pltpu.VMEM)
    density, energy = pl.pallas_call(
        kernel,
        out_shape=(jax.ShapeDtypeStruct((96, 384), F32), jax.ShapeDtypeStruct((1,), F32)),
        in_specs=[smem] * 4 + [pl.BlockSpec(memory_space=pl.ANY)] * 2 + [vmem] * 3,
        out_specs=(vmem, smem),
        scratch_shapes=[
            pltpu.VMEM((4, 8, 512, 256), BF16),
            pltpu.VMEM((1024, 384), BF16),
            pltpu.VMEM((4, 512, 512), BF16),
            pltpu.VMEM((64, 256, 256), BF16),
            pltpu.VMEM((384, 1024), BF16),
            pltpu.VMEM((3, 384, 256), BF16),
            pltpu.VMEM((8, 256), I32),
            pltpu.VMEM((2, 8, 256), I32),
            pltpu.VMEM((8, 2, 256, 256), BF16),
            pltpu.VMEM((8, 2, 256, 256), BF16),
            pltpu.VMEM((8, 2, 384, 256), BF16),
            pltpu.VMEM((8, 2, 384, 256), BF16),
            pltpu.VMEM((8, 2, 4, 48, 384), F32),
            pltpu.VMEM((8, 4, 48, 384), F32),
            pltpu.VMEM((8, 4, 48, 384), BF16),
            pltpu.VMEM((8, 3, 48, 384), BF16),
            pltpu.VMEM((8, 48, 384), F32),
            pltpu.VMEM((8, 48, 384), BF16),
            pltpu.VMEM((7, 48, 384), BF16),
            pltpu.VMEM((8, 48, 384), BF16),
            pltpu.VMEM((4, 16, 384), F32),
            pltpu.VMEM((3, 16, 384), F32),
            pltpu.VMEM((8, 2, 384), F32),
            pltpu.VMEM((7, 2, 384), F32),
            pltpu.VMEM((8, 8, 2, 384), F32),
            DMA((4,)), DMA,
            DMA((2,)), DMA((2,)),
            DMA((8,)), DMA((8,)),
            DMA((8,)), DMA((8,)),
            DMA((8,)), DMA((8,)),
            DMA((8,)), DMA((8,)),
            DMA((8, 3)), DMA((8, 3)),
            DMA((8,)), DMA((7,)),
            DMA((7,)), DMA((8,)),
            DMA((3,)), DMA((3,)),
            DMA((7,)), DMA((7,)),
            DMA((7,)), DMA((8,)),
            DMA((7,)), DMA((8,)),
        ],
        compiler_params=pltpu.CompilerParams(
            collective_id=0, has_side_effects=True, vmem_limit_bytes=56 << 20
        ),
    )(
        block_ids.T, block_count, occ_pick, occ_energy,
        ints, vir_coef.reshape(1024, 384), occ_coef, occ_pick.reshape(1, 512), vir_energy,
    )
    return (energy, density)


def solution(mesh):
    placed = (P("aux", "pair", None, None), P("pair", None), P("pair"), P(), P(), P(), P(), P())
    return jax.shard_map(
        per_device,
        mesh=mesh,
        in_specs=placed,
        out_specs=(P("aux"), P("pair", None)),
        check_vma=False,
    )
```

time: 156 us -> 137 us (0.88)
  Pallas kernels: 149 us -> 132 us
  local copies, waits for them, and re-layouts: 4.16 us -> 1.58 us
    pallas_call x1, Pallas kernels: 149 us -> 132 us  [per_device(): pl.pallas_call(kernel, out_shape=(jax.ShapeDtypeStruct((96, 384), F32), j...]
where the time goes in v2:
time: 137 us
  Pallas kernels  132 us (96%)
  between operations  3.04 us (2%)
  local copies, waits for them, and re-layouts  1.58 us (1%)
    pallas_call x1, Pallas kernels, per_device(): pl.pallas_call(kernel, out_shape=(jax.ShapeDtypeStruct((96, 384), F32), j...  132 us

profile of v2, /device:TPU:1, one launch (start us, length us, event | category | flops | bytes accessed | tf_op | source)
XLA Modules:
  0.0 137.0 jit_solution(1774855125594755691)
XLA Ops:
  1.3 132.4 %shard_map.95 = (f32[96,384]{1,0:T(8,128)}, f32[1]{0:T(128)}) custom-call(s32[2,4]{1,0:T(2,128)} %bitcast.9, s32[1]{0:T(128)S(6)} %copy.12.count, s32[512]{0:T(512)} %pick_s.1, f32[512]{0:T(512)} %eocc.1, bf16[4,8,512,256]{3,2,1,0:T(8,128)(2,1)} %bitcast.6, bf16[1024,384]{1,0:T(8,128)(2,1)} %bitcast.7, bf16[16,64,512]{2,1,0:T(8,128)(2,1)} %occ.1, ...), custom_call_target="tpu_custom_call" | custom-call | tf_op jit(solution)/shard_map/pallas_call | solution.py:348
  134.3 1.6 %copy.14 = f32[96,384]{1,0:T(8,128)} copy(f32[96,384]{1,0:T(8,128)} %get-tuple-element.9) | data formatting | bytes 294912

commit v3 on v2

--- a/solution.py
+++ b/solution.py
@@ -27,16 +27,17 @@
 
 
 def kernel(
-    ids, count, pick_s, eocc,
-    ints_hbm, vir_hbm, occ, pick_v, evir,
+    ids, count,
+    ints_hbm, vir_hbm, occ_hbm, pick_hbm, eocc_hbm, evir_hbm,
     out_d, out_e,
-    ints, vir, lhs, half, vir_t, vt, meta, meta_in,
+    ints, vir, occ, pick, eocc, evir, lhs, half, vir_t, vt, meta, meta_in,
     far, near, relay, part,
     cbuf, core_in, x_out, x_in, zsum, z_out, z_in, call,
-    dblk, d_in, dy, zr_in, fin,
-    ints_sem, vir_sem, meta_ss, meta_rs, far_ss, far_rs, near_ss, near_rs, part_ss, part_rs,
+    dblk, d_in, line_in, fin,
+    load_sem, met,
+    meta_ss, meta_rs, far_ss, far_rs, near_ss, near_rs, part_ss, part_rs,
     core_ss, core_rs, x_ss, x_rs, z_ss, z_rs, ag_ss, ag_rs, y_ss, y_rs,
-    zr_ss, zr_rs, zg_ss, zg_rs, f_ss, f_rs,
+    line_ss, line_rs, f_ss, f_rs,
 ):
     a = lax.axis_index("aux")
     p = lax.axis_index("pair")
@@ -55,33 +56,26 @@
     def ypeer(step):
         return dev(x, lax.rem(p + step + NY, NY), z, c)
 
-    loads = [pltpu.make_async_copy(ints_hbm.at[s], ints.at[s], ints_sem.at[s]) for s in range(4)]
-    for load in loads:
+    barrier = pltpu.get_barrier_semaphore()
+    beside = [
+        dev(x, p, z, 1 - c),
+        dev(lax.rem(x + 1, NX), p, z, c),
+        dev(lax.rem(x + NX - 1, NX), p, z, c),
+        dev(x, p, lax.rem(z + 1, NZ), c),
+        dev(x, p, lax.rem(z + NZ - 1, NZ), c),
+    ]
+    for to in [ypeer(1), ypeer(-1)] + beside:
+        pl.semaphore_signal(barrier, inc=1, device_id=to, device_id_type=MESH)
+
+    small = [
+        pltpu.make_async_copy(src, dst, load_sem.at[i])
+        for i, (src, dst) in enumerate(
+            ((pick_hbm, pick), (occ_hbm, occ), (eocc_hbm, eocc), (evir_hbm, evir), (vir_hbm, vir))
+        )
+    ]
+    loads = [pltpu.make_async_copy(ints_hbm.at[s], ints.at[s], load_sem.at[5 + s]) for s in range(4)]
+    for load in small[:2] + loads + small[2:]:
         load.start()
-    vir_load = pltpu.make_async_copy(vir_hbm, vir, vir_sem)
-    vir_load.start()
-
-    barrier = pltpu.get_barrier_semaphore()
-
-    def greet(to):
-        pl.semaphore_signal(barrier, inc=1, device_id=to, device_id_type=MESH)
-
-    for step in range(1, NY):
-        greet(ypeer(step))
-
-    def greet_xc(o, carry):
-        s = lax.rem(x * NC + c + o, NX * NC)
-        greet(dev(lax.div(s, NC), p, z, lax.rem(s, NC)))
-        return carry
-
-    lax.fori_loop(1, NX * NC, greet_xc, 0)
-
-    def greet_z(o, carry):
-        pz = lax.rem(z + o, NZ)
-        greet(dev(x, p, pz, c))
-        return carry
-
-    lax.fori_loop(1, NZ, greet_z, 0)
 
     lane = iota((8, 256), 1)
     slot = lax.shift_right_logical(lane, 6)
@@ -90,7 +84,9 @@
         mine = jnp.where(slot == k, ids[0, k], mine)
     meta[...] = jnp.where(slot < count[0], mine * 64 + (lane & 63), -1)
 
-    pick_t = onehot(iota((512, 64), 0) == pick_v[:, 0:64])
+    small[0].wait()
+    small[1].wait()
+    pick_t = onehot(iota((512, 64), 0) == pick[:, 0:64])
     rows = jnp.concatenate([occ[ids[1, s]] for s in range(4)], axis=0)
     chosen = dot(rows, pick_t).astype(BF16)
     r = iota((512, 64), 0)
@@ -102,7 +98,7 @@
         tiled = jnp.concatenate([chosen[s * 64 : s * 64 + 64]] * 8, axis=0)
         lhs[s] = jnp.where(same, dot(spread, tiled, NT), 0.0).astype(BF16)
 
-    pl.semaphore_wait(barrier, 3 + 7 + 7)
+    pl.semaphore_wait(barrier, 7)
 
     metas = [
         remote(meta, meta_in.at[0], meta_ss.at[0], meta_rs.at[0], ypeer(-1)),
@@ -144,7 +140,13 @@
     half_rows(0, 16)
     half_rows(16, 48)
 
-    vir_load.wait()
+    for r in range(3):
+        for to in beside:
+            pl.semaphore_signal(met.at[r], inc=1, device_id=to, device_id_type=MESH)
+        pl.semaphore_wait(met.at[r], 5)
+
+    for load in small[2:]:
+        load.wait()
     vir_t[...] = vir[...].astype(F32).T.astype(BF16)
     row = iota((1024, 256), 0)
     vt[0] = dot(vir_t[...], onehot(row == meta[0:1, :])).astype(BF16)
@@ -246,7 +248,11 @@
         ag_copy(o, lax.rem(slab + o, NX * NC)).wait_recv()
 
     k = p * NZ + z
-    level = eocc[pick_s[k]] + eocc[pick_s[k + 32]]
+    where = iota((1, 512), 1)
+    level = 0.0
+    for g in (k, k + 32):
+        orbital = jnp.sum(jnp.where(where == g, pick[...], 0))
+        level = level + jnp.sum(jnp.where(where == orbital, eocc[...], 0.0))
     block = call[...].astype(F32).reshape(384, 384)
     block_t = block.T
     across = jnp.broadcast_to(evir[...].reshape(1, 384), (384, 384))
@@ -264,7 +270,7 @@
     plain = (((1,), (0,)), ((), ()))
     share = high(high(chosen, 2.0 * amplitude - amplitude_t, plain), amplitude_t, plain)
     share = share + high(high(chosen, 2.0 * amplitude_t - amplitude, plain), amplitude, plain)
-    share = share + jnp.where((iota((64, 384), 1) == k) & (rank == 12), energy, 0.0)
+    share = share + jnp.where((iota((64, 384), 1) == k) & ((rank == 12) | (rank == 13)), energy, 0.0)
     for y in range(4):
         dblk[y] = share[y * 16 : y * 16 + 16]
 
@@ -278,38 +284,34 @@
     for o in range(1, NY):
         y_copy(o).wait_recv()
         total = total + d_in[o - 1]
-    dy[...] = total.reshape(8, 2, 384)
-
-    def zr_copy(o):
+    rest = total - total.astype(BF16).astype(F32)
+    line_in[z] = jnp.where(iota((16, 384), 0) == 13, rest, total).astype(BF16)
+
+    def line_copy(o, src):
         pz = lax.rem(z + o, NZ)
-        return remote(dy.at[pz], zr_in.at[o - 1], zr_ss.at[o - 1], zr_rs.at[o - 1], dev(x, p, pz, c))
-
-    def zg_copy(o, src):
-        pz = lax.rem(z + o, NZ)
-        return remote(fin.at[slab, src], fin.at[slab, src], zg_ss.at[o - 1], zg_rs.at[src], dev(x, p, pz, c))
+        return remote(line_in.at[src], line_in.at[src], line_ss.at[o - 1], line_rs.at[src], dev(x, p, pz, c))
 
     def f_copy(o, src):
         to = lax.rem(slab + o, NX * NC)
         return remote(fin.at[src], fin.at[src], f_ss.at[o - 1], f_rs.at[src], dev(lax.div(to, NC), p, z, lax.rem(to, NC)))
 
+    for o in (4, 3, 5, 2, 6, 1, 7):
+        line_copy(o, z).start()
     for o in range(1, NZ):
-        zr_copy(o).start()
-    total = dy[z]
+        line_copy(o, lax.rem(z + o, NZ)).wait_recv()
+    total = line_in[0].astype(F32)
     for o in range(1, NZ):
-        zr_copy(o).wait_recv()
-        total = total + zr_in[o - 1]
-    fin[slab, z] = total
-    for o in range(1, NZ):
-        zg_copy(o, z).start()
-    for o in range(1, NZ):
-        zg_copy(o, lax.rem(z + o, NZ)).wait_recv()
-    for o in range(1, NX * NC):
+        total = total + line_in[o].astype(F32)
+    fin[slab] = total
+    for o in (4, 5, 3, 2, 6, 1, 7):
         f_copy(o, slab).start()
     for o in range(1, NX * NC):
         f_copy(o, lax.rem(slab + o, NX * NC)).wait_recv()
 
-    out_d[...] = fin[:, 0:6].reshape(96, 384)
-    out_e[0] = jnp.sum(jnp.where(iota((1, 384), 1) == lax.rem(a, 32), fin[0, 6][0:1, :], 0.0))
+    for s in range(NX * NC):
+        out_d[s * 12 : s * 12 + 12, :] = fin[s, 0:12]
+    energies = fin[0, 12:13] + fin[0, 13:14]
+    out_e[0] = jnp.sum(jnp.where(iota((1, 384), 1) == lax.rem(a, 32), energies, 0.0))
 
     for m in metas:
         m.wait_send()
@@ -335,8 +337,7 @@
     for o in range(1, NY):
         y_copy(o).wait_send()
     for o in range(1, NZ):
-        zr_copy(o).wait_send()
-        zg_copy(o, z).wait_send()
+        line_copy(o, z).wait_send()
 
 
 def per_device(
@@ -348,11 +349,15 @@
     density, energy = pl.pallas_call(
         kernel,
         out_shape=(jax.ShapeDtypeStruct((96, 384), F32), jax.ShapeDtypeStruct((1,), F32)),
-        in_specs=[smem] * 4 + [pl.BlockSpec(memory_space=pl.ANY)] * 2 + [vmem] * 3,
+        in_specs=[smem] * 2 + [pl.BlockSpec(memory_space=pl.ANY)] * 6,
         out_specs=(vmem, smem),
         scratch_shapes=[
             pltpu.VMEM((4, 8, 512, 256), BF16),
             pltpu.VMEM((1024, 384), BF16),
+            pltpu.VMEM((16, 64, 512), BF16),
+            pltpu.VMEM((1, 512), I32),
+            pltpu.VMEM((1, 512), F32),
+            pltpu.VMEM((384,), F32),
             pltpu.VMEM((4, 512, 512), BF16),
             pltpu.VMEM((64, 256, 256), BF16),
             pltpu.VMEM((384, 1024), BF16),
@@ -373,10 +378,9 @@
             pltpu.VMEM((8, 48, 384), BF16),
             pltpu.VMEM((4, 16, 384), F32),
             pltpu.VMEM((3, 16, 384), F32),
-            pltpu.VMEM((8, 2, 384), F32),
-            pltpu.VMEM((7, 2, 384), F32),
-            pltpu.VMEM((8, 8, 2, 384), F32),
-            DMA((4,)), DMA,
+            pltpu.VMEM((8, 16, 384), BF16),
+            pltpu.VMEM((8, 16, 384), F32),
+            DMA((9,)), pltpu.SemaphoreType.REGULAR((3,)),
             DMA((2,)), DMA((2,)),
             DMA((8,)), DMA((8,)),
             DMA((8,)), DMA((8,)),
@@ -386,7 +390,6 @@
             DMA((8,)), DMA((7,)),
             DMA((7,)), DMA((8,)),
             DMA((3,)), DMA((3,)),
-            DMA((7,)), DMA((7,)),
             DMA((7,)), DMA((8,)),
             DMA((7,)), DMA((8,)),
         ],
@@ -394,8 +397,8 @@
             collective_id=0, has_side_effects=True, vmem_limit_bytes=56 << 20
         ),
     )(
-        block_ids.T, block_count, occ_pick, occ_energy,
-        ints, vir_coef.reshape(1024, 384), occ_coef, occ_pick.reshape(1, 512), vir_energy,
+        block_ids.T, block_count,
+        ints, vir_coef.reshape(1024, 384), occ_coef, occ_pick.reshape(1, 512), occ_energy.reshape(1, 512), vir_energy,
     )
     return (energy, density)
 

time: 137 us -> 131 us (0.956)
  Pallas kernels: 132 us -> 126 us
    pallas_call x1, Pallas kernels: 132 us -> 126 us  [per_device(): pl.pallas_call(kernel, out_shape=(jax.ShapeDtypeStruct((96, 384), F32), j...]
where the time goes in v3:
time: 131 us
  Pallas kernels  126 us (96%)
  between operations  3.04 us (2%)
  local copies, waits for them, and re-layouts  1.58 us (1%)
    pallas_call x1, Pallas kernels, per_device(): pl.pallas_call(kernel, out_shape=(jax.ShapeDtypeStruct((96, 384), F32), j...  126 us

profile of v3, /device:TPU:1, one launch (start us, length us, event | category | flops | bytes accessed | tf_op | source)
XLA Modules:
  0.0 130.7 jit_solution(12634134953540522390)
XLA Ops:
  1.3 126.1 %shard_map.95 = (f32[96,384]{1,0:T(8,128)}, f32[1]{0:T(128)}) custom-call(s32[2,4]{1,0:T(2,128)} %bitcast.11, s32[1]{0:T(128)S(6)} %copy.12.count, bf16[4,8,512,256]{3,2,1,0:T(8,128)(2,1)} %bitcast.7, bf16[1024,384]{1,0:T(8,128)(2,1)} %bitcast.8, bf16[16,64,512]{2,1,0:T(8,128)(2,1)} %occ_hbm.1, s32[1,512]{1,0:T(1,128)} %bitcast.9, f32[1,512]{1,0:T(1,128)} %bitcast.10, ...), custom_call_target="tpu_custom_call" | custom-call | tf_op jit(solution)/shard_map/pallas_call | solution.py:349
  128.0 1.6 %copy.14 = f32[96,384]{1,0:T(8,128)} copy(f32[96,384]{1,0:T(8,128)} %get-tuple-element.9) | data formatting | bytes 294912

commit v4 on v3

--- a/solution.py
+++ b/solution.py
@@ -29,10 +29,10 @@
 def kernel(
     ids, count,
     ints_hbm, vir_hbm, occ_hbm, pick_hbm, eocc_hbm, evir_hbm,
-    out_d, out_e,
+    out,
     ints, vir, occ, pick, eocc, evir, lhs, half, vir_t, vt, meta, meta_in,
     far, near, relay, part,
-    cbuf, core_in, x_out, x_in, zsum, z_out, z_in, call,
+    cbuf, core_in, x_out, x_in, zsum, z_out, z_in, call, weight, mix,
     dblk, d_in, line_in, fin,
     load_sem, met,
     meta_ss, meta_rs, far_ss, far_rs, near_ss, near_rs, part_ss, part_rs,
@@ -98,14 +98,10 @@
         tiled = jnp.concatenate([chosen[s * 64 : s * 64 + 64]] * 8, axis=0)
         lhs[s] = jnp.where(same, dot(spread, tiled, NT), 0.0).astype(BF16)
 
-    pl.semaphore_wait(barrier, 7)
-
     metas = [
         remote(meta, meta_in.at[0], meta_ss.at[0], meta_rs.at[0], ypeer(-1)),
         remote(meta, meta_in.at[1], meta_ss.at[1], meta_rs.at[1], ypeer(1)),
     ]
-    for m in metas:
-        m.start()
     for load in loads:
         load.wait()
 
@@ -134,11 +130,16 @@
             return carry
 
         lax.fori_loop(0, 4, one_slot, 0)
-        for j in range(low // 8, (low + n) // 8):
-            far_copy(j).start()
 
     half_rows(0, 16)
+    pl.semaphore_wait(barrier, 7)
+    for m in metas:
+        m.start()
+    for j in range(2):
+        far_copy(j).start()
     half_rows(16, 48)
+    for j in range(2, 8):
+        far_copy(j).start()
 
     for r in range(3):
         for to in beside:
@@ -151,7 +152,7 @@
     row = iota((1024, 256), 0)
     vt[0] = dot(vir_t[...], onehot(row == meta[0:1, :])).astype(BF16)
     for g in range(2):
-        metas[g].wait_recv()
+        metas[g].wait()
         vt[1 + g] = dot(vir_t[...], onehot(row == meta_in[g, 0:1, :])).astype(BF16)
 
     def do_relay(j):
@@ -210,6 +211,18 @@
         def _():
             z_copy(j, lax.rem(z - j + NZ, NZ)).start()
 
+    def sent(j):
+        far_copy(j).wait_send()
+        near_copy(j).wait_send()
+        part_copy(j).wait_send()
+        core_copy(j).wait_send()
+        for o in range(1, NX):
+            x_copy(j, o).wait_send()
+
+        @pl.when(z != j)
+        def _():
+            z_copy(j, 1).wait_send()
+
     def step(n, carry):
         @pl.when(n < 8)
         def _():
@@ -223,6 +236,10 @@
         @pl.when(n > 2)
         def _():
             do_target(n - 3)
+
+        @pl.when(n > 4)
+        def _():
+            sent(n - 5)
 
         return carry
 
@@ -244,35 +261,41 @@
 
     for o in range(1, NX * NC):
         ag_copy(o, slab).start()
-    for o in range(1, NX * NC):
-        ag_copy(o, lax.rem(slab + o, NX * NC)).wait_recv()
-
     k = p * NZ + z
     where = iota((1, 512), 1)
     level = 0.0
     for g in (k, k + 32):
         orbital = jnp.sum(jnp.where(where == g, pick[...], 0))
         level = level + jnp.sum(jnp.where(where == orbital, eocc[...], 0.0))
+    across = jnp.broadcast_to(evir[...].reshape(1, 384), (384, 384))
+    weight[...] = 1.0 / (level - across.T - across)
+    sent(6)
+    sent(7)
+    for o in range(1, NX * NC):
+        ag_copy(o, lax.rem(slab + o, NX * NC)).wait_recv()
+
     block = call[...].astype(F32).reshape(384, 384)
     block_t = block.T
-    across = jnp.broadcast_to(evir[...].reshape(1, 384), (384, 384))
-    denom = level - across.T - across
-    amplitude = block / denom
+    amplitude = block * weight[...]
     energy = jnp.sum(amplitude * (2.0 * block - block_t))
-    amplitude_t = block_t / denom
+    amplitude_t = block_t * weight[...]
 
     high = functools.partial(
-        lax.dot_general, precision=lax.Precision.HIGHEST, preferred_element_type=F32
+        jnp.dot, precision=lax.Precision.HIGHEST, preferred_element_type=F32
     )
-    rank = iota((64, 384), 0) & 15
-    wanted = lax.shift_right_logical(iota((64, 384), 0), 4) * 96 + slab * 12 + rank
-    chosen = jnp.where((iota((64, 384), 1) == wanted) & (rank < 12), 1.0, 0.0)
-    plain = (((1,), (0,)), ((), ()))
-    share = high(high(chosen, 2.0 * amplitude - amplitude_t, plain), amplitude_t, plain)
-    share = share + high(high(chosen, 2.0 * amplitude_t - amplitude, plain), amplitude, plain)
-    share = share + jnp.where((iota((64, 384), 1) == k) & ((rank == 12) | (rank == 13)), energy, 0.0)
+    mix[0] = 2.0 * amplitude - amplitude_t
+    mix[1] = 2.0 * amplitude_t - amplitude
+
+    def mine_of(g):
+        starts = [pl.multiple_of(y * 96 + x * 24, 8) for y in range(4)]
+        return jnp.concatenate([mix[g, pl.ds(start, 24), :] for start in starts], axis=0)
+
+    share = high(mine_of(0), amplitude_t) + high(mine_of(1), amplitude)
+    tip = jnp.where(iota((4, 384), 1) == k, energy, 0.0)
     for y in range(4):
-        dblk[y] = share[y * 16 : y * 16 + 16]
+        lo = y * 24
+        dblk[y, 0:12] = jnp.where(c == 0, share[lo : lo + 12], share[lo + 12 : lo + 24])
+        dblk[y, 12:16] = tip
 
     def y_copy(o):
         y = lax.rem(p + o, NY)
@@ -280,6 +303,8 @@
 
     for o in range(1, NY):
         y_copy(o).start()
+    for o in range(1, NX * NC):
+        ag_copy(o, slab).wait_send()
     total = dblk[p]
     for o in range(1, NY):
         y_copy(o).wait_recv()
@@ -297,6 +322,8 @@
 
     for o in (4, 3, 5, 2, 6, 1, 7):
         line_copy(o, z).start()
+    for o in range(1, NY):
+        y_copy(o).wait_send()
     for o in range(1, NZ):
         line_copy(o, lax.rem(z + o, NZ)).wait_recv()
     total = line_in[0].astype(F32)
@@ -305,39 +332,22 @@
     fin[slab] = total
     for o in (4, 5, 3, 2, 6, 1, 7):
         f_copy(o, slab).start()
+    for o in range(1, NZ):
+        line_copy(o, z).wait_send()
     for o in range(1, NX * NC):
         f_copy(o, lax.rem(slab + o, NX * NC)).wait_recv()
 
+    out[...] = fin[...]
+    for o in range(1, NX * NC):
+        f_copy(o, slab).wait_send()
+
+
+def finish(fin, out_d, out_e):
     for s in range(NX * NC):
         out_d[s * 12 : s * 12 + 12, :] = fin[s, 0:12]
     energies = fin[0, 12:13] + fin[0, 13:14]
-    out_e[0] = jnp.sum(jnp.where(iota((1, 384), 1) == lax.rem(a, 32), energies, 0.0))
-
-    for m in metas:
-        m.wait_send()
-
-    def sent(j, carry):
-        far_copy(j).wait_send()
-        near_copy(j).wait_send()
-        part_copy(j).wait_send()
-        core_copy(j).wait_send()
-        for o in range(1, NX):
-            x_copy(j, o).wait_send()
-
-        @pl.when(z != j)
-        def _():
-            z_copy(j, 1).wait_send()
-
-        return carry
-
-    lax.fori_loop(0, 8, sent, 0)
-    for o in range(1, NX * NC):
-        ag_copy(o, slab).wait_send()
-        f_copy(o, slab).wait_send()
-    for o in range(1, NY):
-        y_copy(o).wait_send()
-    for o in range(1, NZ):
-        line_copy(o, z).wait_send()
+    pair = lax.rem(lax.axis_index("aux"), 32)
+    out_e[0] = jnp.sum(jnp.where(iota((1, 384), 1) == pair, energies, 0.0))
 
 
 def per_device(
@@ -346,11 +356,11 @@
     ints = jnp.transpose(shell_ints, (1, 2, 3, 0)).reshape(4, 8, 512, 256)
     smem = pl.BlockSpec(memory_space=pltpu.SMEM)
     vmem = pl.BlockSpec(memory_space=pltpu.VMEM)
-    density, energy = pl.pallas_call(
+    rows = pl.pallas_call(
         kernel,
-        out_shape=(jax.ShapeDtypeStruct((96, 384), F32), jax.ShapeDtypeStruct((1,), F32)),
+        out_shape=jax.ShapeDtypeStruct((8, 16, 384), F32),
         in_specs=[smem] * 2 + [pl.BlockSpec(memory_space=pl.ANY)] * 6,
-        out_specs=(vmem, smem),
+        out_specs=vmem,
         scratch_shapes=[
             pltpu.VMEM((4, 8, 512, 256), BF16),
             pltpu.VMEM((1024, 384), BF16),
@@ -376,6 +386,8 @@
             pltpu.VMEM((8, 48, 384), BF16),
             pltpu.VMEM((7, 48, 384), BF16),
             pltpu.VMEM((8, 48, 384), BF16),
+            pltpu.VMEM((384, 384), F32),
+            pltpu.VMEM((2, 384, 384), F32),
             pltpu.VMEM((4, 16, 384), F32),
             pltpu.VMEM((3, 16, 384), F32),
             pltpu.VMEM((8, 16, 384), BF16),
@@ -400,6 +412,12 @@
         block_ids.T, block_count,
         ints, vir_coef.reshape(1024, 384), occ_coef, occ_pick.reshape(1, 512), occ_energy.reshape(1, 512), vir_energy,
     )
+    density, energy = pl.pallas_call(
+        finish,
+        out_shape=(jax.ShapeDtypeStruct((96, 384), F32), jax.ShapeDtypeStruct((1,), F32)),
+        in_specs=[vmem],
+        out_specs=(vmem, smem),
+    )(rows)
     return (energy, density)
 
 

time: 131 us -> 128 us (0.977)
  between operations: 3.04 us -> 1.29 us
  local copies, waits for them, and re-layouts: 1.58 us -> 0 us
    unnamed x1 -> x0, local copies, waits for them, and re-layouts: 1.58 us -> none
    pallas_call x1 -> x2, Pallas kernels: 126 us -> 126 us  [the longest x1 125 us: per_device(): pl.pallas_call(kernel, out_shape=jax.ShapeDtypeStruct((8, 16, 384), F32),...]
where the time goes in v4:
time: 128 us
  Pallas kernels  126 us (98%)
  between operations  1.29 us (1%)
    pallas_call x1, Pallas kernels, per_device(): pl.pallas_call(kernel, out_shape=jax.ShapeDtypeStruct((8, 16, 384), F32),...  125 us

profile of v4, /device:TPU:1, one launch (start us, length us, event | category | flops | bytes accessed | tf_op | source)
XLA Modules:
  0.0 127.8 jit_solution(10273166053079618953)
XLA Ops:
  1.3 124.9 %shard_map.95.fin = f32[8,16,384]{2,1,0:T(8,128)} custom-call(s32[2,4]{1,0:T(2,128)} %bitcast.11, s32[1]{0:T(128)S(6)} %copy.10.count, bf16[4,8,512,256]{3,2,1,0:T(8,128)(2,1)} %bitcast.7, bf16[1024,384]{1,0:T(8,128)(2,1)} %bitcast.8, bf16[16,64,512]{2,1,0:T(8,128)(2,1)} %occ_hbm.1, s32[1,512]{1,0:T(1,128)} %bitcast.9, f32[1,512]{1,0:T(1,128)} %bitcast.10, ...), custom_call_target="tpu_custom_call" | custom-call | tf_op jit(solution)/shard_map/pallas_call | solution.py:359
  126.2 1.6 %shard_map.96 = (f32[96,384]{1,0:T(8,128)}, f32[1]{0:T(128)}) custom-call(f32[8,16,384]{2,1,0:T(8,128)} %shard_map.95.fin), custom_call_target="tpu_custom_call" | custom-call | tf_op jit(solution)/shard_map/pallas_call | solution.py:415
